TPU v7x, 32 devices: a whole 2x2x4 slice. The times are simulated.
32 devices in a mesh: gx: 4 (over x, core), gy: 8 (over z, y).
Axes of the slice: x: 2, y: 2, z: 4, core: 2. Of those that a mesh axis runs over, the one named last changes fastest.
Arguments:
- volume: bfloat16 [16, 64, 16, 128], P('gx', 'gy'), may hold values from -6 to 6
- basin_mask: int32 [16, 64, 32], P('gx', 'gy'), may hold values 0 or 1
- w_first: bfloat16 [27, 64, 128], replicated, may hold values from -0.15625 to 0.15625
- b_first: float32 [128], replicated, may hold values from -3 to 3
- w_second: bfloat16 [27, 128, 128], replicated, may hold values from -0.109375 to 0.109375
- b_second: float32 [128], replicated, may hold values from -3 to 3
- upstream: bfloat16 [16, 64, 32, 128], P('gx', 'gy'), may hold values from -6 to 6
Outputs:
- features: bfloat16 [16, 64, 32, 128], P('gx', 'gy')
- step_first: float32 [27, 64, 128], replicated
- step_second: float32 [27, 128, 128], replicated
Inputs may be any that keep to these rules, and one draw needn't show every extreme that they name: basin_mask holds only 0 and 1.
All inputs are finite; a program needn't handle non-finite values. No bound on the sum of `basin_mask` on one device may be relied on, other than what follows from the above.
Results may differ from a plain program's by a relative error of at most 0.0054.
Values may be sent and summed in bfloat16 or wider, within the bound.
No kernel may reach another device: no remote copies, remote signals or barrier semaphores. Data moves between devices by JAX's collectives and lax.ppermute only.
A program may use at most 64 MiB of HBM per device.

v0:
```python
import jax
import jax.numpy as jnp
from jax import lax
from jax.sharding import PartitionSpec as P


def extended_2(block, sides, width):
    for axis, dim in sides:
        count = lax.axis_size(axis)
        forward = [(i, i + 1) for i in range(count - 1)]
        backward = [(target, source) for source, target in forward]
        low = lax.ppermute(
            lax.slice_in_dim(block, block.shape[dim] - width, None, axis=dim), axis, forward
        )
        high = lax.ppermute(lax.slice_in_dim(block, 0, width, axis=dim), axis, backward)
        block = jnp.concatenate([low, block, high], axis=dim)
    return block


def pad_depth(extended):
    return jnp.pad(extended, ((0, 0), (0, 0), (1, 1), (0, 0)))


def group_window(padded, tap_x, tap_y, cells_x, cells_y, cells_z):
    parts = [
        padded[tap_x : tap_x + cells_x, tap_y : tap_y + cells_y, tap_z : tap_z + cells_z]
        for tap_z in range(3)
    ]
    joined = jnp.concatenate(parts, axis=-1)
    return joined.reshape(cells_x * cells_y * cells_z, joined.shape[3])


def convolve(padded, weights, cells_x, cells_y, cells_z):
    chan_in = weights.shape[1]
    total = jnp.zeros((cells_x * cells_y * cells_z, weights.shape[2]), jnp.float32)
    for tap_x in range(3):
        for tap_y in range(3):
            window = group_window(padded, tap_x, tap_y, cells_x, cells_y, cells_z)
            first = 9 * tap_x + 3 * tap_y
            kernel = weights[first : first + 3].reshape(3 * chan_in, weights.shape[2])
            total = total + jnp.dot(window, kernel, preferred_element_type=jnp.float32)
    return total


def weight_grad(padded, grad, cells_x, cells_y, cells_z):
    pieces = []
    for tap_x in range(3):
        for tap_y in range(3):
            window = group_window(padded, tap_x, tap_y, cells_x, cells_y, cells_z)
            product = lax.dot_general(
                window, grad, (((0,), (0,)), ((), ())), preferred_element_type=jnp.float32
            )
            pieces.append(product.reshape(3, padded.shape[3], grad.shape[1]))
    return jnp.concatenate(pieces, axis=0)


def normalized_with(grad, total, count):
    return grad * lax.rsqrt(total / count + 1e-06)


def on_device(volume, basin_mask, w_first, b_first, w_second, b_second, upstream):
    cells_x, cells_y, half_z, doubled = volume.shape
    chan_in = doubled // 2
    cells_z = 2 * half_z
    chan_out = w_first.shape[2]
    field = volume.reshape(cells_x, cells_y, cells_z, chan_in)
    active = basin_mask.astype(jnp.float32).reshape(-1, 1)
    padded_in = pad_depth(extended_2(field, (("gx", 0), ("gy", 1)), 1))
    pre_first = convolve(padded_in, w_first, cells_x, cells_y, cells_z) + b_first
    sig_first = jax.nn.sigmoid(pre_first)
    hidden = (
        (pre_first * sig_first * active)
        .astype(jnp.bfloat16)
        .reshape(cells_x, cells_y, cells_z, chan_out)
    )
    padded_hidden = pad_depth(extended_2(hidden, (("gx", 0), ("gy", 1)), 1))
    pre_second = convolve(padded_hidden, w_second, cells_x, cells_y, cells_z) + b_second
    sig_second = jax.nn.sigmoid(pre_second)
    features = (
        (pre_second * sig_second * active)
        .astype(jnp.bfloat16)
        .reshape(cells_x, cells_y, cells_z, chan_out)
    )
    grad_second = (
        upstream.reshape(-1, chan_out).astype(jnp.float32)
        * active
        * sig_second
        * (1.0 + pre_second * (1.0 - sig_second))
    ).astype(jnp.bfloat16)
    dw_second = weight_grad(padded_hidden, grad_second, cells_x, cells_y, cells_z)
    flipped = jnp.transpose(w_second[::-1], (0, 2, 1))
    grad_field = grad_second.reshape(cells_x, cells_y, cells_z, chan_out)
    padded_grad = pad_depth(extended_2(grad_field, (("gx", 0), ("gy", 1)), 1))
    back_hidden = convolve(padded_grad, flipped, cells_x, cells_y, cells_z)
    grad_first = (back_hidden * active * sig_first * (1.0 + pre_first * (1.0 - sig_first))).astype(
        jnp.bfloat16
    )
    dw_first = weight_grad(padded_in, grad_first, cells_x, cells_y, cells_z)
    count_first = float(dw_first.size)
    count_second = float(dw_second.size)
    sum_first, sum_second = lax.psum((dw_first, dw_second), ("gx", "gy"))
    step_first = normalized_with(sum_first, jnp.sum(sum_first * sum_first), count_first)
    step_second = normalized_with(sum_second, jnp.sum(sum_second * sum_second), count_second)
    return (features, step_first, step_second)


def solution(mesh):
    in_specs = (
        P("gx", "gy", None, None),
        P("gx", "gy", None),
        P(),
        P(),
        P(),
        P(),
        P("gx", "gy", None, None),
    )
    out_specs = (P("gx", "gy", None, None), P(), P())
    return jax.shard_map(
        on_device, mesh=mesh, in_specs=in_specs, out_specs=out_specs, check_vma=False
    )
```

profile of v0, /device:TPU:0, one launch (start us, length us, event | category | flops | bytes accessed | tf_op | source)
XLA Modules:
  0.0 280.9 jit_solution(11516559743100319684)
XLA Ops:
  8.2 2.4 collective-permute-start
  10.7 1.4 collective-permute-start.1
  12.1 2.2 fusion.62
  15.1 1.3 copy.31
  16.6 4.2 %collective-permute-start.2 = (bf16[6,1,32,64]{3,2,1,0:T(8,128)(2,1)S(1)}, bf16[6,1,32,64]{3,2,1,0:T(8,128)(2,1)S(1)}, u32[]{:S(2)}, u32[]{:S(2)}) collective-permute-start(bf16[6,1,32,64]{3,2,1,0:T(8,128)(2,1)S(1)} %get-tuple-element.116), channel_id=1, source_target_pairs={{0,1},{1,2},{2,3},{3,4},{4,5},{5,6},{6,7},{8,9},{9,10},{10,11},{11... | collective-permute-start | bytes 73736 | tf_op jit(solution)/shard_map/ppermute | solution.py:12
  20.8 1.3 collective-permute-start.3
  24.0 2.9 %collective-permute-done.3 = bf16[6,1,32,64]{3,2,1,0:T(8,128)(2,1)S(1)} collective-permute-done((bf16[6,1,32,64]{3,2,1,0:T(8,128)(2,1)S(1)}, bf16[6,1,32,64]{3,2,1,0:T(8,128)(2,1)S(1)}, u32[]{:S(2)}, u32[]{:S(2)}) %collective-permute-start.3) | collective-permute-done | bytes 24608 | tf_op jit(solution)/shard_map/ppermute | solution.py:15
  34.0 3.0 %collective-permute-start.4 = (bf16[1,8,32,128]{3,2,1,0:T(8,128)(2,1)S(1)}, bf16[1,8,32,128]{3,2,1,0:T(8,128)(2,1)S(1)}, u32[]{:S(2)}, u32[]{:S(2)}) collective-permute-start(bf16[1,8,32,128]{3,2,1,0:T(8,128)(2,1)S(1)} %bitcast.334), channel_id=1, source_target_pairs={{0,8},{8,16},{16,24},{1,9},{9,17},{17,25},{2,10},{10,18},{18,26},{... | collective-permute-start | bytes 196616 | tf_op jit(solution)/shard_map/ppermute | solution.py:12
  37.0 1.3 collective-permute-start.5
  39.3 3.5 %collective-permute-done.5 = bf16[1,8,32,128]{3,2,1,0:T(8,128)(2,1)S(1)} collective-permute-done((bf16[1,8,32,128]{3,2,1,0:T(8,128)(2,1)S(1)}, bf16[1,8,32,128]{3,2,1,0:T(8,128)(2,1)S(1)}, u32[]{:S(2)}, u32[]{:S(2)}) %collective-permute-start.5) | collective-permute-done | bytes 65568 | tf_op jit(solution)/shard_map/ppermute | solution.py:15
  43.5 5.0 %collective-permute-start.6 = (bf16[6,1,32,128]{3,2,1,0:T(8,128)(2,1)}, bf16[6,1,32,128]{3,2,1,0:T(8,128)(2,1)}, u32[]{:S(2)}, u32[]{:S(2)}) collective-permute-start(bf16[6,1,32,128]{3,2,1,0:T(8,128)(2,1)} %get-tuple-element.110), channel_id=1, source_target_pairs={{0,1},{1,2},{2,3},{3,4},{4,5},{5,6},{6,7},{8,9},{9,10},{10,11},{11... | collective-permute-start | bytes 147464 | tf_op jit(solution)/shard_map/ppermute | solution.py:12
  48.4 1.5 collective-permute-start.7
  51.0 2.0 copy.30
  63.6 1.7 fusion.64
  67.6 2.1 fusion.76
  79.3 2.3 copy.47
  81.6 1.7 convolution_add_fusion.15
  91.7 4.7 %collective-permute-start.8 = (bf16[1,8,32,128]{3,2,1,0:T(8,128)(2,1)}, bf16[1,8,32,128]{3,2,1,0:T(8,128)(2,1)S(1)}, u32[]{:S(2)}, u32[]{:S(2)}) collective-permute-start(bf16[1,8,32,128]{3,2,1,0:T(8,128)(2,1)} %bitcast.45), channel_id=1, source_target_pairs={{0,8},{8,16},{16,24},{1,9},{9,17},{17,25},{2,10},{10,18},{18,26},{... | collective-permute-start | bytes 196616 | tf_op jit(solution)/shard_map/ppermute | solution.py:12
  96.4 1.5 collective-permute-start.9
  105.7 4.3 %collective-permute-start.10 = (bf16[6,1,32,128]{3,2,1,0:T(8,128)(2,1)S(1)}, bf16[6,1,32,128]{3,2,1,0:T(8,128)(2,1)S(1)}, u32[]{:S(2)}, u32[]{:S(2)}) collective-permute-start(bf16[6,1,32,128]{3,2,1,0:T(8,128)(2,1)S(1)} %get-tuple-element.106), channel_id=1, source_target_pairs={{0,1},{1,2},{2,3},{3,4},{4,5},{5,6},{6,7},{8,9},{9,10},{10,11},{11... | collective-permute-start | bytes 147464 | tf_op jit(solution)/shard_map/ppermute | solution.py:12
  112.3 4.1 %collective-permute-done.11 = bf16[6,1,32,128]{3,2,1,0:T(8,128)(2,1)S(1)} collective-permute-done((bf16[6,1,32,128]{3,2,1,0:T(8,128)(2,1)S(1)}, bf16[6,1,32,128]{3,2,1,0:T(8,128)(2,1)S(1)}, u32[]{:S(2)}, u32[]{:S(2)}) %collective-permute-start.11) | collective-permute-done | bytes 49184 | tf_op jit(solution)/shard_map/ppermute | solution.py:15
  128.5 138.2 %all-reduce.6.cloned.1.call-done = (f32[27,64,128]{2,1,0:T(8,128)}, f32[27,128,128]{2,1,0:T(8,128)}) async-done(((f32[27,64,128]{2,1,0:T(8,128)}, f32[27,128,128]{2,1,0:T(8,128)}), (f32[27,64,128]{2,1,0:T(8,128)}, f32[27,128,128]{2,1,0:T(8,128)})) %all-reduce.6.cloned.1.call-update) | async-done | bytes 2654224 | tf_op jit(solution)/shard_map/psum | solution.py:101
  266.7 2.7 multiply_reduce_fusion
  270.1 1.3 broadcast_multiply_fusion
  (250 shorter events, 67.9 us)
Async XLA Ops:
  7.2 7.8 %copy-start.37 = (bf16[4,8,16,128]{3,2,1,0:T(8,128)(2,1)S(1)}, bf16[4,8,16,128]{3,2,1,0:T(8,128)(2,1)}, u32[]{:S(2)}) copy-start(bf16[4,8,16,128]{3,2,1,0:T(8,128)(2,1)} %param.7) | copy-start | bytes 393220
  7.2 7.1 %copy-start.38 = (bf16[27,64,128]{2,1,0:T(8,128)(2,1)S(1)}, bf16[27,64,128]{2,1,0:T(8,128)(2,1)}, u32[]{:S(2)}) copy-start(bf16[27,64,128]{2,1,0:T(8,128)(2,1)} %param.9) | copy-start | bytes 1327108
  7.2 259.5 %all-reduce.6.cloned.1.call-start = ((), (), s32[]{:S(2)}) async-start(), calls=%async_computation | async-start | bytes 5308416 | tf_op jit(solution)/shard_map/psum | solution.py:101
  8.2 8.3 %collective-permute-start = (bf16[1,8,32,64]{3,2,1,0:T(8,128)(2,1)S(1)}, bf16[1,8,32,64]{3,2,1,0:T(8,128)(2,1)S(1)}, u32[]{:S(2)}, u32[]{:S(2)}) collective-permute-start(bf16[1,8,32,64]{3,2,1,0:T(8,128)(2,1)S(1)} %slice.487), channel_id=1, source_target_pairs={{0,8},{8,16},{16,24},{1,9},{9,17},{17,25},{2,10},{10,18},{18,26},{... | collective-permute-start | bytes 98312 | tf_op jit(solution)/shard_map/ppermute | solution.py:12
  10.6 4.6 %copy-start.4 = (bf16[27,128,128]{2,1,0:T(8,128)(2,1)S(1)}, bf16[27,128,128]{2,1,0:T(8,128)(2,1)}, u32[]{:S(2)}) copy-start(bf16[27,128,128]{2,1,0:T(8,128)(2,1)} %param.11) | copy-start | bytes 2654212
  10.7 5.9 %collective-permute-start.1 = (bf16[1,8,32,64]{3,2,1,0:T(8,128)(2,1)S(1)}, bf16[1,8,32,64]{3,2,1,0:T(8,128)(2,1)S(1)}, u32[]{:S(2)}, u32[]{:S(2)}) collective-permute-start(bf16[1,8,32,64]{3,2,1,0:T(8,128)(2,1)S(1)} %slice.489), channel_id=1, source_target_pairs={{8,0},{16,8},{24,16},{9,1},{17,9},{25,17},{10,2},{18,10},{26,18},{... | collective-permute-start | bytes 98312 | tf_op jit(solution)/shard_map/ppermute | solution.py:15
  16.5 6.8 %copy-start.58 = (s32[4,8,32]{2,1,0:T(8,128)S(1)}, s32[4,8,32]{2,1,0:T(8,128)}, u32[]{:S(2)}) copy-start(s32[4,8,32]{2,1,0:T(8,128)} %param.8) | copy-start | bytes 12292
  16.6 7.4 %collective-permute-start.2 = (bf16[6,1,32,64]{3,2,1,0:T(8,128)(2,1)S(1)}, bf16[6,1,32,64]{3,2,1,0:T(8,128)(2,1)S(1)}, u32[]{:S(2)}, u32[]{:S(2)}) collective-permute-start(bf16[6,1,32,64]{3,2,1,0:T(8,128)(2,1)S(1)} %get-tuple-element.116), channel_id=1, source_target_pairs={{0,1},{1,2},{2,3},{3,4},{4,5},{5,6},{6,7},{8,9},{9,10},{10,11},{11... | collective-permute-start | bytes 73736 | tf_op jit(solution)/shard_map/ppermute | solution.py:12
  20.8 6.0 %collective-permute-start.3 = (bf16[6,1,32,64]{3,2,1,0:T(8,128)(2,1)S(1)}, bf16[6,1,32,64]{3,2,1,0:T(8,128)(2,1)S(1)}, u32[]{:S(2)}, u32[]{:S(2)}) collective-permute-start(bf16[6,1,32,64]{3,2,1,0:T(8,128)(2,1)S(1)} %get-tuple-element.117), channel_id=1, source_target_pairs={{1,0},{2,1},{3,2},{4,3},{5,4},{6,5},{7,6},{9,8},{10,9},{11,10},{12... | collective-permute-start | bytes 73736 | tf_op jit(solution)/shard_map/ppermute | solution.py:15
  23.3 8.1 %copy-start.15 = (bf16[1024,64]{1,0:T(8,128)(2,1)}, bf16[1024,64]{1,0:T(8,128)(2,1)S(1)}, u32[]{:S(2)}) copy-start(bf16[1024,64]{1,0:T(8,128)(2,1)S(1)} %concatenate.198) | copy-start | bytes 393220
  32.9 5.5 %copy-start.5 = (bf16[27,128,128]{2,1,0:T(8,128)(2,1)S(1)}, bf16[27,128,128]{2,1,0:T(8,128)(2,1)}, u32[]{:S(2)}) copy-start(bf16[27,128,128]{2,1,0:T(8,128)(2,1)} %reverse_bitcast_fusion) | copy-start | bytes 2654212
  34.0 15.9 %copy-start.16 = (bf16[1024,64]{1,0:T(8,128)(2,1)S(1)}, bf16[1024,64]{1,0:T(8,128)(2,1)}, u32[]{:S(2)}) copy-start(bf16[1024,64]{1,0:T(8,128)(2,1)} %copy-done.15) | copy-start | bytes 393220
  34.0 5.3 %collective-permute-start.4 = (bf16[1,8,32,128]{3,2,1,0:T(8,128)(2,1)S(1)}, bf16[1,8,32,128]{3,2,1,0:T(8,128)(2,1)S(1)}, u32[]{:S(2)}, u32[]{:S(2)}) collective-permute-start(bf16[1,8,32,128]{3,2,1,0:T(8,128)(2,1)S(1)} %bitcast.334), channel_id=1, source_target_pairs={{0,8},{8,16},{16,24},{1,9},{9,17},{17,25},{2,10},{10,18},{18,26},{... | collective-permute-start | bytes 196616 | tf_op jit(solution)/shard_map/ppermute | solution.py:12
  37.0 5.8 %collective-permute-start.5 = (bf16[1,8,32,128]{3,2,1,0:T(8,128)(2,1)S(1)}, bf16[1,8,32,128]{3,2,1,0:T(8,128)(2,1)S(1)}, u32[]{:S(2)}, u32[]{:S(2)}) collective-permute-start(bf16[1,8,32,128]{3,2,1,0:T(8,128)(2,1)S(1)} %bitcast.333), channel_id=1, source_target_pairs={{8,0},{16,8},{24,16},{9,1},{17,9},{25,17},{10,2},{18,10},{26,18},{... | collective-permute-start | bytes 196616 | tf_op jit(solution)/shard_map/ppermute | solution.py:15
  43.5 17.2 %collective-permute-start.6 = (bf16[6,1,32,128]{3,2,1,0:T(8,128)(2,1)}, bf16[6,1,32,128]{3,2,1,0:T(8,128)(2,1)}, u32[]{:S(2)}, u32[]{:S(2)}) collective-permute-start(bf16[6,1,32,128]{3,2,1,0:T(8,128)(2,1)} %get-tuple-element.110), channel_id=1, source_target_pairs={{0,1},{1,2},{2,3},{3,4},{4,5},{5,6},{6,7},{8,9},{9,10},{10,11},{11... | collective-permute-start | bytes 147464 | tf_op jit(solution)/shard_map/ppermute | solution.py:12
  48.4 12.2 %collective-permute-start.7 = (bf16[6,1,32,128]{3,2,1,0:T(8,128)(2,1)}, bf16[6,1,32,128]{3,2,1,0:T(8,128)(2,1)}, u32[]{:S(2)}, u32[]{:S(2)}) collective-permute-start(bf16[6,1,32,128]{3,2,1,0:T(8,128)(2,1)} %get-tuple-element.111), channel_id=1, source_target_pairs={{1,0},{2,1},{3,2},{4,3},{5,4},{6,5},{7,6},{9,8},{10,9},{11,10},{12... | collective-permute-start | bytes 147464 | tf_op jit(solution)/shard_map/ppermute | solution.py:15
  79.3 4.1 %copy-start.49 = (bf16[3,128,128]{2,1,0:T(8,128)(2,1)S(1)}, bf16[3,128,128]{2,1,0:T(8,128)(2,1)}, u32[]{:S(2)}) copy-start(bf16[3,128,128]{2,1,0:T(8,128)(2,1)} %get-tuple-element.20) | copy-start | bytes 294916
  88.8 9.1 %copy-start.8 = (bf16[1024,384]{0,1:T(8,128)(2,1)S(1)}, bf16[1024,384]{0,1:T(8,128)(2,1)}, u32[]{:S(2)}) copy-start(bf16[1024,384]{0,1:T(8,128)(2,1)} %copy.41) | copy-start | bytes 2359300
  90.6 8.5 %copy-start.9 = (bf16[1024,384]{0,1:T(8,128)(2,1)S(1)}, bf16[1024,384]{0,1:T(8,128)(2,1)}, u32[]{:S(2)}) copy-start(bf16[1024,384]{0,1:T(8,128)(2,1)} %copy.42) | copy-start | bytes 2359300
  91.7 8.3 %copy-start.11 = (bf16[1024,384]{0,1:T(8,128)(2,1)S(1)}, bf16[1024,384]{0,1:T(8,128)(2,1)}, u32[]{:S(2)}) copy-start(bf16[1024,384]{0,1:T(8,128)(2,1)} %copy.43) | copy-start | bytes 2359300
  91.7 13.9 %collective-permute-start.8 = (bf16[1,8,32,128]{3,2,1,0:T(8,128)(2,1)}, bf16[1,8,32,128]{3,2,1,0:T(8,128)(2,1)S(1)}, u32[]{:S(2)}, u32[]{:S(2)}) collective-permute-start(bf16[1,8,32,128]{3,2,1,0:T(8,128)(2,1)} %bitcast.45), channel_id=1, source_target_pairs={{0,8},{8,16},{16,24},{1,9},{9,17},{17,25},{2,10},{10,18},{18,26},{... | collective-permute-start | bytes 196616 | tf_op jit(solution)/shard_map/ppermute | solution.py:12
  96.4 9.2 %collective-permute-start.9 = (bf16[1,8,32,128]{3,2,1,0:T(8,128)(2,1)}, bf16[1,8,32,128]{3,2,1,0:T(8,128)(2,1)S(1)}, u32[]{:S(2)}, u32[]{:S(2)}) collective-permute-start(bf16[1,8,32,128]{3,2,1,0:T(8,128)(2,1)} %bitcast.332), channel_id=1, source_target_pairs={{8,0},{16,8},{24,16},{9,1},{17,9},{25,17},{10,2},{18,10},{26,18},{... | collective-permute-start | bytes 196616 | tf_op jit(solution)/shard_map/ppermute | solution.py:15
  105.7 6.6 %collective-permute-start.10 = (bf16[6,1,32,128]{3,2,1,0:T(8,128)(2,1)S(1)}, bf16[6,1,32,128]{3,2,1,0:T(8,128)(2,1)S(1)}, u32[]{:S(2)}, u32[]{:S(2)}) collective-permute-start(bf16[6,1,32,128]{3,2,1,0:T(8,128)(2,1)S(1)} %get-tuple-element.106), channel_id=1, source_target_pairs={{0,1},{1,2},{2,3},{3,4},{4,5},{5,6},{6,7},{8,9},{9,10},{10,11},{11... | collective-permute-start | bytes 147464 | tf_op jit(solution)/shard_map/ppermute | solution.py:12
  110.0 6.4 %collective-permute-start.11 = (bf16[6,1,32,128]{3,2,1,0:T(8,128)(2,1)S(1)}, bf16[6,1,32,128]{3,2,1,0:T(8,128)(2,1)S(1)}, u32[]{:S(2)}, u32[]{:S(2)}) collective-permute-start(bf16[6,1,32,128]{3,2,1,0:T(8,128)(2,1)S(1)} %get-tuple-element.107), channel_id=1, source_target_pairs={{1,0},{2,1},{3,2},{4,3},{5,4},{6,5},{7,6},{9,8},{10,9},{11,10},{12... | collective-permute-start | bytes 147464 | tf_op jit(solution)/shard_map/ppermute | solution.py:15
  (53 other events, 73.0 us)
Sparse Core Ops, SparseCore 0:
  128.7 138.0 all-reduce.5
where the time goes:
time: 282 us; the launch traced here: 281 us
  waiting for transfers between devices  149 us (53%)
  local copies, waits for them, and re-layouts  40.8 us (14%)
  starting transfers between devices  31.9 us (11%)
  matrix products  25.8 us (9%)
  other arithmetic  17.3 us (6%)
  between operations  16.5 us (6%)
    psum x1, waiting for transfers between devices, on_device(): sum_first, sum_second = lax.psum((dw_first, dw_second), ('gx', 'gy'))  138 us
    ppermute x6, starting transfers between devices, extended_2(): lax.ppermute(lax.slice_in_dim(block, block.shape[dim] - width, None, axis...  23.6 us
    dot_general x27, matrix products, convolve(): total = total + jnp.dot(window, kernel, preferred_element_type=jnp.float32)  14.1 us
    dot_general x18, matrix products, weight_grad(): lax.dot_general(window, grad, (((0,), (0,)), ((), ())), preferred_element...  11.8 us
    dot_general x10, local copies, waits for them, and re-layouts, weight_grad(): lax.dot_general(window, grad, (((0,), (0,)), ((), ())), preferred_element...  10.8 us
    ppermute x6, waiting for transfers between devices, extended_2(): lax.ppermute(lax.slice_in_dim(block, 0, width, axis=dim), axis, backward)  10.4 us
    reshape x8, local copies, waits for them, and re-layouts, group_window(): return joined.reshape(cells_x * cells_y * cells_z, joined.shape[3])  9.72 us
    ppermute x6, starting transfers between devices, extended_2(): lax.ppermute(lax.slice_in_dim(block, 0, width, axis=dim), axis, backward)  8.27 us
  transfers between devices with their start and end apart: 13, of which 4 were waited for; matrix products, arithmetic and copies ran while one was open for 9% of the time, Pallas kernels for 0%

commit v1 on v0

--- a/solution.py
+++ b/solution.py
@@ -2,6 +2,11 @@
 import jax.numpy as jnp
 from jax import lax
 from jax.sharding import PartitionSpec as P
+
+
+def axis_by_axis(x, one, other):
+    half = lax.psum(x, one)
+    return lax.psum(half, other)
 
 
 def extended_2(block, sides, width):
@@ -98,7 +103,7 @@
     dw_first = weight_grad(padded_in, grad_first, cells_x, cells_y, cells_z)
     count_first = float(dw_first.size)
     count_second = float(dw_second.size)
-    sum_first, sum_second = lax.psum((dw_first, dw_second), ("gx", "gy"))
+    sum_first, sum_second = axis_by_axis((dw_first, dw_second), "gy", "gx")
     step_first = normalized_with(sum_first, jnp.sum(sum_first * sum_first), count_first)
     step_second = normalized_with(sum_second, jnp.sum(sum_second * sum_second), count_second)
     return (features, step_first, step_second)

time: 282 us -> 324 us (1.15)
  waiting for transfers between devices: 149 us -> 190 us
    psum x1 -> x2, waiting for transfers between devices: 138 us -> 180 us  [the longest x1 118 us: axis_by_axis(): half = lax.psum(x, one)]
  transfers between devices with their start and end apart: 13 -> 14, of which waited for: 4 -> 5; matrix products, arithmetic and copies ran while one was open for 9% -> 8% of each run, Pallas kernels for 0% -> 0%
where the time goes in v1:
time: 324 us; the launch traced here: 322 us
  waiting for transfers between devices  190 us (59%)
  local copies, waits for them, and re-layouts  40.8 us (13%)
  starting transfers between devices  31.9 us (10%)
  matrix products  25.9 us (8%)
  other arithmetic  17.2 us (5%)
  between operations  16.5 us (5%)
    psum x1, waiting for transfers between devices, axis_by_axis(): half = lax.psum(x, one)  118 us
    psum x1, waiting for transfers between devices, axis_by_axis(): return lax.psum(half, other)  61.9 us
    ppermute x6, starting transfers between devices, extended_2(): lax.ppermute(lax.slice_in_dim(block, block.shape[dim] - width, None, axis...  23.5 us
    dot_general x27, matrix products, convolve(): total = total + jnp.dot(window, kernel, preferred_element_type=jnp.float32)  14.1 us
    dot_general x18, matrix products, weight_grad(): lax.dot_general(window, grad, (((0,), (0,)), ((), ())), preferred_element...  11.8 us
    dot_general x10, local copies, waits for them, and re-layouts, weight_grad(): lax.dot_general(window, grad, (((0,), (0,)), ((), ())), preferred_element...  10.8 us
    ppermute x6, waiting for transfers between devices, extended_2(): lax.ppermute(lax.slice_in_dim(block, 0, width, axis=dim), axis, backward)  10.4 us
    reshape x8, local copies, waits for them, and re-layouts, group_window(): return joined.reshape(cells_x * cells_y * cells_z, joined.shape[3])  9.72 us
  transfers between devices with their start and end apart: 14, of which 5 were waited for; matrix products, arithmetic and copies ran while one was open for 8% of the time, Pallas kernels for 0%

profile of v1, /device:TPU:0, one launch (start us, length us, event | category | flops | bytes accessed | tf_op | source)
XLA Modules:
  0.0 322.4 jit_solution(13862556347170446722)
XLA Ops:
  8.2 2.4 collective-permute-start
  10.7 1.4 collective-permute-start.1
  12.1 2.2 fusion.62
  15.2 1.3 copy.31
  16.6 4.2 %collective-permute-start.2 = (bf16[6,1,32,64]{3,2,1,0:T(8,128)(2,1)S(1)}, bf16[6,1,32,64]{3,2,1,0:T(8,128)(2,1)S(1)}, u32[]{:S(2)}, u32[]{:S(2)}) collective-permute-start(bf16[6,1,32,64]{3,2,1,0:T(8,128)(2,1)S(1)} %get-tuple-element.118), channel_id=1, source_target_pairs={{0,1},{1,2},{2,3},{3,4},{4,5},{5,6},{6,7},{8,9},{9,10},{10,11},{11... | collective-permute-start | bytes 73736 | tf_op jit(solution)/shard_map/ppermute | solution.py:17
  20.9 1.3 collective-permute-start.3
  24.0 2.8 collective-permute-done.3
  34.0 3.0 collective-permute-start.4
  39.4 3.5 %collective-permute-done.5 = bf16[1,8,32,128]{3,2,1,0:T(8,128)(2,1)S(1)} collective-permute-done((bf16[1,8,32,128]{3,2,1,0:T(8,128)(2,1)S(1)}, bf16[1,8,32,128]{3,2,1,0:T(8,128)(2,1)S(1)}, u32[]{:S(2)}, u32[]{:S(2)}) %collective-permute-start.5) | collective-permute-done | bytes 65568 | tf_op jit(solution)/shard_map/ppermute | solution.py:20
  43.5 4.9 %collective-permute-start.6 = (bf16[6,1,32,128]{3,2,1,0:T(8,128)(2,1)}, bf16[6,1,32,128]{3,2,1,0:T(8,128)(2,1)}, u32[]{:S(2)}, u32[]{:S(2)}) collective-permute-start(bf16[6,1,32,128]{3,2,1,0:T(8,128)(2,1)} %get-tuple-element.112), channel_id=1, source_target_pairs={{0,1},{1,2},{2,3},{3,4},{4,5},{5,6},{6,7},{8,9},{9,10},{10,11},{11... | collective-permute-start | bytes 147464 | tf_op jit(solution)/shard_map/ppermute | solution.py:17
  48.5 1.5 collective-permute-start.7
  51.0 2.0 copy.30
  63.6 1.7 fusion.64
  67.5 2.1 fusion.76
  79.3 2.3 copy.47
  81.6 1.7 convolution_add_fusion.15
  91.7 4.7 %collective-permute-start.8 = (bf16[1,8,32,128]{3,2,1,0:T(8,128)(2,1)}, bf16[1,8,32,128]{3,2,1,0:T(8,128)(2,1)S(1)}, u32[]{:S(2)}, u32[]{:S(2)}) collective-permute-start(bf16[1,8,32,128]{3,2,1,0:T(8,128)(2,1)} %bitcast.45), channel_id=1, source_target_pairs={{0,8},{8,16},{16,24},{1,9},{9,17},{17,25},{2,10},{10,18},{18,26},{... | collective-permute-start | bytes 196616 | tf_op jit(solution)/shard_map/ppermute | solution.py:17
  96.4 1.5 collective-permute-start.9
  105.6 4.3 %collective-permute-start.10 = (bf16[6,1,32,128]{3,2,1,0:T(8,128)(2,1)S(1)}, bf16[6,1,32,128]{3,2,1,0:T(8,128)(2,1)S(1)}, u32[]{:S(2)}, u32[]{:S(2)}) collective-permute-start(bf16[6,1,32,128]{3,2,1,0:T(8,128)(2,1)S(1)} %get-tuple-element.108), channel_id=1, source_target_pairs={{0,1},{1,2},{2,3},{3,4},{4,5},{5,6},{6,7},{8,9},{9,10},{10,11},{11... | collective-permute-start | bytes 147464 | tf_op jit(solution)/shard_map/ppermute | solution.py:17
  112.3 4.1 %collective-permute-done.11 = bf16[6,1,32,128]{3,2,1,0:T(8,128)(2,1)S(1)} collective-permute-done((bf16[6,1,32,128]{3,2,1,0:T(8,128)(2,1)S(1)}, bf16[6,1,32,128]{3,2,1,0:T(8,128)(2,1)S(1)}, u32[]{:S(2)}, u32[]{:S(2)}) %collective-permute-start.11) | collective-permute-done | bytes 49184 | tf_op jit(solution)/shard_map/ppermute | solution.py:20
  128.5 117.8 %all-reduce.8.cloned.1.call-done = (f32[27,64,128]{2,1,0:T(8,128)}, f32[27,128,128]{2,1,0:T(8,128)}) async-done(((f32[27,64,128]{2,1,0:T(8,128)}, f32[27,128,128]{2,1,0:T(8,128)}), (f32[27,64,128]{2,1,0:T(8,128)}, f32[27,128,128]{2,1,0:T(8,128)})) %all-reduce.8.cloned.1.call-update) | async-done | bytes 2654224 | tf_op jit(solution)/shard_map/psum | solution.py:8
  246.4 61.9 %all-reduce.10.cloned.1.call-done = (f32[27,64,128]{2,1,0:T(8,128)}, f32[27,128,128]{2,1,0:T(8,128)}) async-done(((f32[27,64,128]{2,1,0:T(8,128)}, f32[27,128,128]{2,1,0:T(8,128)}), (f32[27,64,128]{2,1,0:T(8,128)}, f32[27,128,128]{2,1,0:T(8,128)})) %all-reduce.10.cloned.1.call-update) | async-done | bytes 2654224 | tf_op jit(solution)/shard_map/psum | solution.py:9
  308.3 2.7 multiply_reduce_fusion
  311.7 1.3 broadcast_multiply_fusion
  (253 shorter events, 69.2 us)
Async XLA Ops:
  7.2 7.8 %copy-start.37 = (bf16[4,8,16,128]{3,2,1,0:T(8,128)(2,1)S(1)}, bf16[4,8,16,128]{3,2,1,0:T(8,128)(2,1)}, u32[]{:S(2)}) copy-start(bf16[4,8,16,128]{3,2,1,0:T(8,128)(2,1)} %param.7) | copy-start | bytes 393220
  7.2 7.2 %copy-start.38 = (bf16[27,64,128]{2,1,0:T(8,128)(2,1)S(1)}, bf16[27,64,128]{2,1,0:T(8,128)(2,1)}, u32[]{:S(2)}) copy-start(bf16[27,64,128]{2,1,0:T(8,128)(2,1)} %param.9) | copy-start | bytes 1327108
  7.2 239.1 %all-reduce.8.cloned.1.call-start = ((), (), s32[]{:S(2)}) async-start(), calls=%async_computation | async-start | bytes 5308416 | tf_op jit(solution)/shard_map/psum | solution.py:8
  8.2 8.3 %collective-permute-start = (bf16[1,8,32,64]{3,2,1,0:T(8,128)(2,1)S(1)}, bf16[1,8,32,64]{3,2,1,0:T(8,128)(2,1)S(1)}, u32[]{:S(2)}, u32[]{:S(2)}) collective-permute-start(bf16[1,8,32,64]{3,2,1,0:T(8,128)(2,1)S(1)} %slice.487), channel_id=1, source_target_pairs={{0,8},{8,16},{16,24},{1,9},{9,17},{17,25},{2,10},{10,18},{18,26},{... | collective-permute-start | bytes 98312 | tf_op jit(solution)/shard_map/ppermute | solution.py:17
  10.6 4.6 %copy-start.4 = (bf16[27,128,128]{2,1,0:T(8,128)(2,1)S(1)}, bf16[27,128,128]{2,1,0:T(8,128)(2,1)}, u32[]{:S(2)}) copy-start(bf16[27,128,128]{2,1,0:T(8,128)(2,1)} %param.11) | copy-start | bytes 2654212
  10.7 5.9 %collective-permute-start.1 = (bf16[1,8,32,64]{3,2,1,0:T(8,128)(2,1)S(1)}, bf16[1,8,32,64]{3,2,1,0:T(8,128)(2,1)S(1)}, u32[]{:S(2)}, u32[]{:S(2)}) collective-permute-start(bf16[1,8,32,64]{3,2,1,0:T(8,128)(2,1)S(1)} %slice.489), channel_id=1, source_target_pairs={{8,0},{16,8},{24,16},{9,1},{17,9},{25,17},{10,2},{18,10},{26,18},{... | collective-permute-start | bytes 98312 | tf_op jit(solution)/shard_map/ppermute | solution.py:20
  16.5 6.8 %copy-start.58 = (s32[4,8,32]{2,1,0:T(8,128)S(1)}, s32[4,8,32]{2,1,0:T(8,128)}, u32[]{:S(2)}) copy-start(s32[4,8,32]{2,1,0:T(8,128)} %param.8) | copy-start | bytes 12292
  16.6 7.4 %collective-permute-start.2 = (bf16[6,1,32,64]{3,2,1,0:T(8,128)(2,1)S(1)}, bf16[6,1,32,64]{3,2,1,0:T(8,128)(2,1)S(1)}, u32[]{:S(2)}, u32[]{:S(2)}) collective-permute-start(bf16[6,1,32,64]{3,2,1,0:T(8,128)(2,1)S(1)} %get-tuple-element.118), channel_id=1, source_target_pairs={{0,1},{1,2},{2,3},{3,4},{4,5},{5,6},{6,7},{8,9},{9,10},{10,11},{11... | collective-permute-start | bytes 73736 | tf_op jit(solution)/shard_map/ppermute | solution.py:17
  20.9 6.0 %collective-permute-start.3 = (bf16[6,1,32,64]{3,2,1,0:T(8,128)(2,1)S(1)}, bf16[6,1,32,64]{3,2,1,0:T(8,128)(2,1)S(1)}, u32[]{:S(2)}, u32[]{:S(2)}) collective-permute-start(bf16[6,1,32,64]{3,2,1,0:T(8,128)(2,1)S(1)} %get-tuple-element.119), channel_id=1, source_target_pairs={{1,0},{2,1},{3,2},{4,3},{5,4},{6,5},{7,6},{9,8},{10,9},{11,10},{12... | collective-permute-start | bytes 73736 | tf_op jit(solution)/shard_map/ppermute | solution.py:20
  23.3 8.1 %copy-start.15 = (bf16[1024,64]{1,0:T(8,128)(2,1)}, bf16[1024,64]{1,0:T(8,128)(2,1)S(1)}, u32[]{:S(2)}) copy-start(bf16[1024,64]{1,0:T(8,128)(2,1)S(1)} %concatenate.198) | copy-start | bytes 393220
  32.9 5.5 %copy-start.5 = (bf16[27,128,128]{2,1,0:T(8,128)(2,1)S(1)}, bf16[27,128,128]{2,1,0:T(8,128)(2,1)}, u32[]{:S(2)}) copy-start(bf16[27,128,128]{2,1,0:T(8,128)(2,1)} %reverse_bitcast_fusion) | copy-start | bytes 2654212
  34.0 15.9 %copy-start.16 = (bf16[1024,64]{1,0:T(8,128)(2,1)S(1)}, bf16[1024,64]{1,0:T(8,128)(2,1)}, u32[]{:S(2)}) copy-start(bf16[1024,64]{1,0:T(8,128)(2,1)} %copy-done.15) | copy-start | bytes 393220
  34.0 5.3 %collective-permute-start.4 = (bf16[1,8,32,128]{3,2,1,0:T(8,128)(2,1)S(1)}, bf16[1,8,32,128]{3,2,1,0:T(8,128)(2,1)S(1)}, u32[]{:S(2)}, u32[]{:S(2)}) collective-permute-start(bf16[1,8,32,128]{3,2,1,0:T(8,128)(2,1)S(1)} %bitcast.334), channel_id=1, source_target_pairs={{0,8},{8,16},{16,24},{1,9},{9,17},{17,25},{2,10},{10,18},{18,26},{... | collective-permute-start | bytes 196616 | tf_op jit(solution)/shard_map/ppermute | solution.py:17
  37.1 5.8 %collective-permute-start.5 = (bf16[1,8,32,128]{3,2,1,0:T(8,128)(2,1)S(1)}, bf16[1,8,32,128]{3,2,1,0:T(8,128)(2,1)S(1)}, u32[]{:S(2)}, u32[]{:S(2)}) collective-permute-start(bf16[1,8,32,128]{3,2,1,0:T(8,128)(2,1)S(1)} %bitcast.333), channel_id=1, source_target_pairs={{8,0},{16,8},{24,16},{9,1},{17,9},{25,17},{10,2},{18,10},{26,18},{... | collective-permute-start | bytes 196616 | tf_op jit(solution)/shard_map/ppermute | solution.py:20
  43.5 17.1 %collective-permute-start.6 = (bf16[6,1,32,128]{3,2,1,0:T(8,128)(2,1)}, bf16[6,1,32,128]{3,2,1,0:T(8,128)(2,1)}, u32[]{:S(2)}, u32[]{:S(2)}) collective-permute-start(bf16[6,1,32,128]{3,2,1,0:T(8,128)(2,1)} %get-tuple-element.112), channel_id=1, source_target_pairs={{0,1},{1,2},{2,3},{3,4},{4,5},{5,6},{6,7},{8,9},{9,10},{10,11},{11... | collective-permute-start | bytes 147464 | tf_op jit(solution)/shard_map/ppermute | solution.py:17
  48.5 12.2 %collective-permute-start.7 = (bf16[6,1,32,128]{3,2,1,0:T(8,128)(2,1)}, bf16[6,1,32,128]{3,2,1,0:T(8,128)(2,1)}, u32[]{:S(2)}, u32[]{:S(2)}) collective-permute-start(bf16[6,1,32,128]{3,2,1,0:T(8,128)(2,1)} %get-tuple-element.113), channel_id=1, source_target_pairs={{1,0},{2,1},{3,2},{4,3},{5,4},{6,5},{7,6},{9,8},{10,9},{11,10},{12... | collective-permute-start | bytes 147464 | tf_op jit(solution)/shard_map/ppermute | solution.py:20
  88.8 9.1 %copy-start.8 = (bf16[1024,384]{0,1:T(8,128)(2,1)S(1)}, bf16[1024,384]{0,1:T(8,128)(2,1)}, u32[]{:S(2)}) copy-start(bf16[1024,384]{0,1:T(8,128)(2,1)} %copy.41) | copy-start | bytes 2359300
  90.5 8.5 %copy-start.9 = (bf16[1024,384]{0,1:T(8,128)(2,1)S(1)}, bf16[1024,384]{0,1:T(8,128)(2,1)}, u32[]{:S(2)}) copy-start(bf16[1024,384]{0,1:T(8,128)(2,1)} %copy.42) | copy-start | bytes 2359300
  91.7 8.4 %copy-start.11 = (bf16[1024,384]{0,1:T(8,128)(2,1)S(1)}, bf16[1024,384]{0,1:T(8,128)(2,1)}, u32[]{:S(2)}) copy-start(bf16[1024,384]{0,1:T(8,128)(2,1)} %copy.43) | copy-start | bytes 2359300
  91.7 13.9 %collective-permute-start.8 = (bf16[1,8,32,128]{3,2,1,0:T(8,128)(2,1)}, bf16[1,8,32,128]{3,2,1,0:T(8,128)(2,1)S(1)}, u32[]{:S(2)}, u32[]{:S(2)}) collective-permute-start(bf16[1,8,32,128]{3,2,1,0:T(8,128)(2,1)} %bitcast.45), channel_id=1, source_target_pairs={{0,8},{8,16},{16,24},{1,9},{9,17},{17,25},{2,10},{10,18},{18,26},{... | collective-permute-start | bytes 196616 | tf_op jit(solution)/shard_map/ppermute | solution.py:17
  96.4 9.2 %collective-permute-start.9 = (bf16[1,8,32,128]{3,2,1,0:T(8,128)(2,1)}, bf16[1,8,32,128]{3,2,1,0:T(8,128)(2,1)S(1)}, u32[]{:S(2)}, u32[]{:S(2)}) collective-permute-start(bf16[1,8,32,128]{3,2,1,0:T(8,128)(2,1)} %bitcast.332), channel_id=1, source_target_pairs={{8,0},{16,8},{24,16},{9,1},{17,9},{25,17},{10,2},{18,10},{26,18},{... | collective-permute-start | bytes 196616 | tf_op jit(solution)/shard_map/ppermute | solution.py:20
  105.6 6.6 %collective-permute-start.10 = (bf16[6,1,32,128]{3,2,1,0:T(8,128)(2,1)S(1)}, bf16[6,1,32,128]{3,2,1,0:T(8,128)(2,1)S(1)}, u32[]{:S(2)}, u32[]{:S(2)}) collective-permute-start(bf16[6,1,32,128]{3,2,1,0:T(8,128)(2,1)S(1)} %get-tuple-element.108), channel_id=1, source_target_pairs={{0,1},{1,2},{2,3},{3,4},{4,5},{5,6},{6,7},{8,9},{9,10},{10,11},{11... | collective-permute-start | bytes 147464 | tf_op jit(solution)/shard_map/ppermute | solution.py:17
  109.9 6.4 %collective-permute-start.11 = (bf16[6,1,32,128]{3,2,1,0:T(8,128)(2,1)S(1)}, bf16[6,1,32,128]{3,2,1,0:T(8,128)(2,1)S(1)}, u32[]{:S(2)}, u32[]{:S(2)}) collective-permute-start(bf16[6,1,32,128]{3,2,1,0:T(8,128)(2,1)S(1)} %get-tuple-element.109), channel_id=1, source_target_pairs={{1,0},{2,1},{3,2},{4,3},{5,4},{6,5},{7,6},{9,8},{10,9},{11,10},{12... | collective-permute-start | bytes 147464 | tf_op jit(solution)/shard_map/ppermute | solution.py:20
  128.5 179.8 %all-reduce.10.cloned.1.call-start = ((), (), s32[]{:S(2)}) async-start(), calls=%async_computation.1 | async-start | bytes 5308416 | tf_op jit(solution)/shard_map/psum | solution.py:9
  (54 other events, 77.0 us)
Sparse Core Ops, SparseCore 0:
  128.6 117.6 all-reduce.7
  248.7 59.4 all-reduce.9
